TPU v7x, 256 devices: a whole 4x4x8 slice. The times are simulated.
256 devices in a mesh: copy: 4 (over x_hi, core), space: 64 (over y, z, x_lo).
Axes of the slice: x: 4 (x_hi: 2, x_lo: 2; x = x_hi * 2 + x_lo), y: 4, z: 8, core: 2. Of those that a mesh axis runs over, the one named last changes fastest.
Arguments:
- noisy_tokens: bfloat16 [4, 256, 256, 384], P('copy', 'space'), may hold values from -6 to 6
- grad_out: bfloat16 [4, 256, 256, 384], P('copy', 'space'), may hold values from -6 to 6
- filter_weight: bfloat16 [2, 256, 256, 384], P(None, None, 'space'), may hold values from -4 to 4
- weight_in: bfloat16 [384, 1536], replicated, may hold values from -0.3125 to 0.3125
- weight_out: bfloat16 [1536, 384], replicated, may hold values from -0.15625 to 0.15625
- gain_one: float32 [384], replicated, may hold values from 0.1 to 1.9
- gain_two: float32 [384], replicated, may hold values from 0.1 to 1.9
Outputs:
- block_out: bfloat16 [4, 256, 256, 384], P('copy', 'space')
- grad_tokens: bfloat16 [4, 256, 256, 384], P('copy', 'space')
- grad_filter: float32 [2, 256, 256, 384], P(None, None, 'space')
- grad_weight_in: bfloat16 [384, 1536], replicated
- grad_weight_out: bfloat16 [1536, 384], replicated
- grad_gain_one: float32 [384], replicated
- grad_gain_two: float32 [384], replicated
All inputs are finite; a program needn't handle non-finite values.
Results may differ from a plain program's by a relative error of at most 0.024.
Values may be sent and summed in bfloat16 or wider, within the bound.
A program may use at most 128 MiB of HBM per device.

v0:
```python
import math
import jax
import jax.numpy as jnp
from jax import lax
from jax.sharding import PartitionSpec as P

EPS = 1e-06


def dft_parts(length):
    index = jnp.arange(length, dtype=jnp.int32)
    phase = index[:, None] * index[None, :] % length
    angle = phase.astype(jnp.float32) * (2.0 * math.pi / length)
    factor = 1.0 / math.sqrt(length)
    return (
        (jnp.cos(angle) * factor).astype(jnp.bfloat16),
        (jnp.sin(angle) * factor).astype(jnp.bfloat16),
    )


def row_table(length):
    cosine, sine = dft_parts(length)
    return jnp.stack([cosine, -sine])


def column_table(length, direction):
    cosine, sine = dft_parts(length)
    upper = jnp.stack([cosine, direction * sine], axis=1)
    lower = jnp.stack([-direction * sine, cosine], axis=1)
    return jnp.stack([upper, lower])


def layer_norm(values):
    centre = jnp.mean(values, axis=-1, keepdims=True)
    centred = values - centre
    variance = jnp.mean(centred * centred, axis=-1, keepdims=True)
    rstd_value = lax.rsqrt(variance + EPS)
    return (centred * rstd_value, rstd_value)


def norm_backward(upstream, normed, rstd_value, gain):
    scaled = upstream * gain
    result = (
        scaled
        - jnp.mean(scaled, axis=-1, keepdims=True)
        - normed * jnp.mean(scaled * normed, axis=-1, keepdims=True)
    ) * rstd_value
    lead = tuple(range(upstream.ndim - 1))
    return (result, jnp.sum(upstream * normed, axis=lead))


def apply_filter(spectrum, filter_weight, direction):
    real_part = spectrum[0].astype(jnp.float32)
    imag_part = spectrum[1].astype(jnp.float32)
    kernel_real = filter_weight[0].astype(jnp.float32)
    kernel_imag = direction * filter_weight[1].astype(jnp.float32)
    return jnp.stack(
        [
            kernel_real * real_part - kernel_imag * imag_part,
            kernel_real * imag_part + kernel_imag * real_part,
        ]
    )


def exact_gelu(values):
    return jax.nn.gelu(values, approximate=False)


def spectral(values, filter_weight, direction):
    width = values.shape[2]
    rows_tab = row_table(width)
    rows = jnp.einsum(
        "pkw,bhwc->pbhkc", rows_tab, values, preferred_element_type=jnp.float32
    ).astype(jnp.bfloat16)
    columns = lax.all_to_all(rows, "space", split_axis=3, concat_axis=2, tiled=True)
    height = columns.shape[2]
    spectrum = jnp.einsum(
        "qmph,pbhkc->qbmkc", column_table(height, 1), columns, preferred_element_type=jnp.float32
    ).astype(jnp.bfloat16)
    weighted = apply_filter(spectrum, filter_weight[:, None], direction).astype(jnp.bfloat16)
    returned = jnp.einsum(
        "qmph,pbhkc->qbmkc", column_table(height, -1), weighted, preferred_element_type=jnp.float32
    ).astype(jnp.bfloat16)
    back_rows = lax.all_to_all(returned, "space", split_axis=2, concat_axis=3, tiled=True)
    output = jnp.einsum("pkw,pbhkc->bhwc", rows_tab, back_rows, preferred_element_type=jnp.float32)
    return (output, spectrum)


def body(noisy_tokens, grad_out, filter_weight, weight_in, weight_out, gain_one, gain_two):
    batch, rows_dev, width, chans = noisy_tokens.shape
    inputs = noisy_tokens.astype(jnp.float32)
    normed_one, rstd_one = layer_norm(inputs)
    mixed_in = (normed_one * gain_one).astype(jnp.bfloat16)
    spatial, spectrum = spectral(mixed_in, filter_weight, 1)
    normed_two, rstd_two = layer_norm(spatial)
    mlp_in = (normed_two * gain_two).astype(jnp.bfloat16).reshape(-1, chans)
    preact = jnp.dot(mlp_in, weight_in, preferred_element_type=jnp.float32)
    activated = exact_gelu(preact).astype(jnp.bfloat16)
    mlp_out = jnp.dot(activated, weight_out, preferred_element_type=jnp.float32)
    block_out = (inputs + mlp_out.reshape(inputs.shape)).astype(jnp.bfloat16)
    upstream = grad_out.reshape(-1, chans)
    grad_act = jnp.dot(upstream, weight_out.T, preferred_element_type=jnp.float32)
    grad_pre = jax.vjp(exact_gelu, preact)[1](grad_act)[0].astype(jnp.bfloat16)
    sum_out = jnp.dot(activated.T, upstream, preferred_element_type=jnp.float32)
    sum_in = jnp.dot(mlp_in.T, grad_pre, preferred_element_type=jnp.float32)
    grad_mlp = jnp.dot(grad_pre, weight_in.T, preferred_element_type=jnp.float32).reshape(
        inputs.shape
    )
    grad_spatial, sum_gain_two = norm_backward(grad_mlp, normed_two, rstd_two, gain_two)
    back_spatial, adjoint = spectral(grad_spatial.astype(jnp.bfloat16), filter_weight, -1)
    spec_f = spectrum.astype(jnp.float32)
    adj_f = adjoint.astype(jnp.float32)
    filter_terms = jnp.stack(
        [
            jnp.sum(adj_f[0] * spec_f[0] + adj_f[1] * spec_f[1], axis=0),
            jnp.sum(adj_f[1] * spec_f[0] - adj_f[0] * spec_f[1], axis=0),
        ]
    )
    grad_filter = lax.psum(filter_terms.astype(jnp.bfloat16), "copy").astype(jnp.float32)
    grad_normed, sum_gain_one = norm_backward(back_spatial, normed_one, rstd_one, gain_one)
    grad_tokens = (grad_out.astype(jnp.float32) + grad_normed).astype(jnp.bfloat16)
    local_sums = (sum_in, sum_out, sum_gain_one, sum_gain_two)
    summed = lax.psum(
        (local_sums[0], local_sums[1], local_sums[2], local_sums[3]), ("copy", "space")
    )
    total_tokens = batch * lax.axis_size("copy") * rows_dev * lax.axis_size("space") * width
    factor = 1.0 / math.sqrt(total_tokens)
    return (
        block_out,
        grad_tokens,
        grad_filter,
        (summed[0] * factor).astype(jnp.bfloat16),
        (summed[1] * factor).astype(jnp.bfloat16),
        summed[2] * factor,
        summed[3] * factor,
    )


def solution(mesh):
    return jax.shard_map(
        body,
        mesh=mesh,
        in_specs=(
            P("copy", "space", None, None),
            P("copy", "space", None, None),
            P(None, None, "space", None),
            P(),
            P(),
            P(),
            P(),
        ),
        out_specs=(
            P("copy", "space", None, None),
            P("copy", "space", None, None),
            P(None, None, "space", None),
            P(),
            P(),
            P(),
            P(),
        ),
        check_vma=False,
    )
```

profile of v0, /device:TPU:1, one launch (start us, length us, event | category | flops | bytes accessed | tf_op | source)
XLA Modules:
  0.0 629.1 jit_solution(3767009619410764740)
XLA Ops:
  13.5 3.0 copy.69
  16.5 13.8 %all-to-all-start = ((bf16[2,1,4,256,384]{4,0,2,1,3:T(2,128)(2,1)}), bf16[2,1,4,256,384]{4,0,2,1,3:T(2,128)(2,1)}, u32[]{:S(2)}, u32[]{:S(2)}) async-start(bf16[2,1,4,256,384]{4,0,2,1,3:T(2,128)(2,1)} %copy.69), calls=%async_computation | async-start | bytes 3145728 | tf_op jit(solution)/shard_map/all_to_all | solution.py:75
  38.8 29.9 %all-to-all-done = bf16[2,1,4,256,384]{4,0,2,1,3:T(2,128)(2,1)} async-done(((bf16[2,1,4,256,384]{4,0,2,1,3:T(2,128)(2,1)}), bf16[2,1,4,256,384]{4,0,2,1,3:T(2,128)(2,1)}, u32[]{:S(2)}, u32[]{:S(2)}) %all-to-all-start) | async-done | bytes 1572896 | tf_op jit(solution)/shard_map/all_to_all | solution.py:75
  77.6 4.3 copy.77
  81.9 45.2 %all_to_all.60 = bf16[2,1,256,4,384]{4,0,3,1,2:T(2,128)(2,1)S(1)} all-to-all(bf16[2,1,256,4,384]{4,0,3,1,2:T(2,128)(2,1)S(1)} %copy.77), channel_id=1, replica_groups=mesh['copy'=4,'space'=64] {'space'}, dimensions={2} | all-to-all | bytes 3145728 | tf_op jit(solution)/shard_map/all_to_all | solution.py:84
  133.1 15.5 %multiply_convert_fusion = (bf16[1024,1536]{1,0:T(8,128)(2,1)}, f32[1024,1536]{1,0:T(8,128)S(1)}, f32[1024,1536]{1,0:T(8,128)S(1)}) fusion(bf16[1024,384]{1,0:T(8,128)(2,1)S(1)} %bitcast.255, bf16[384,1536]{1,0:T(8,128)(2,1)S(1)} %copy-done), kind=kOutput, calls=%fused_computation.3 | convolution fusion | flops 1310195712 | bytes 17694720 | tf_op jit(solution)/shard_map/dot_general | solution.py:97
  148.6 3.3 add_convert_fusion
  157.4 4.0 fusion.40
  161.3 4.9 copy.84
  166.2 7.7 %all-to-all-start.2 = ((bf16[2,1,4,256,384]{4,0,2,1,3:T(2,128)(2,1)}), bf16[2,1,4,256,384]{4,0,2,1,3:T(2,128)(2,1)S(1)}, u32[]{:S(2)}, u32[]{:S(2)}) async-start(bf16[2,1,4,256,384]{4,0,2,1,3:T(2,128)(2,1)} %copy.84), calls=%async_computation.2 | async-start | bytes 3145728 | tf_op jit(solution)/shard_map/all_to_all | solution.py:75
  174.2 5.2 fusion.98
  179.3 3.2 fusion.99
  182.6 31.1 %all-to-all-done.2 = bf16[2,1,4,256,384]{4,0,2,1,3:T(2,128)(2,1)S(1)} async-done(((bf16[2,1,4,256,384]{4,0,2,1,3:T(2,128)(2,1)}), bf16[2,1,4,256,384]{4,0,2,1,3:T(2,128)(2,1)S(1)}, u32[]{:S(2)}, u32[]{:S(2)}) %all-to-all-start.2) | async-done | bytes 1572896 | tf_op jit(solution)/shard_map/all_to_all | solution.py:75
  217.5 4.3 fusion.96
  223.9 3.1 copy.90
  227.0 8.3 %all-to-all-start.3 = ((bf16[2,1,256,4,384]{4,0,3,1,2:T(2,128)(2,1)}), bf16[2,1,256,4,384]{4,0,3,1,2:T(2,128)(2,1)S(1)}, u32[]{:S(2)}, u32[]{:S(2)}) async-start(bf16[2,1,256,4,384]{4,0,3,1,2:T(2,128)(2,1)} %copy.90), calls=%async_computation.3 | async-start | bytes 3145728 | tf_op jit(solution)/shard_map/all_to_all | solution.py:84
  235.6 3.4 fusion.57
  244.7 5.1 fusion.97
  249.8 3.1 copy.81
  252.9 215.0 %all-reduce.7.cloned.1.call-done = (f32[384,1536]{1,0:T(8,128)}, f32[1536,384]{1,0:T(8,128)}) async-done(((f32[384,1536]{1,0:T(8,128)}, f32[1536,384]{1,0:T(8,128)}), (f32[384,1536]{1,0:T(8,128)}, f32[1536,384]{1,0:T(8,128)})) %all-reduce.7.cloned.1.call-update) | async-done | bytes 4718608 | tf_op jit(solution)/shard_map/psum | solution.py:123
  472.0 55.6 %all-reduce.5.cloned.1.call-done = bf16[2,256,4,384]{1,3,2,0:T(8,128)(2,1)} async-done(((bf16[2,256,4,384]{1,3,2,0:T(8,128)(2,1)}), bf16[2,256,4,384]{1,3,2,0:T(8,128)(2,1)}) %all-reduce.5.cloned.1.call-update) | async-done | bytes 1572880 | tf_op jit(solution)/shard_map/psum | solution.py:119
  527.7 3.9 copy.100
  535.7 76.1 %all-reduce = (f32[384]{0:T(512)}, f32[384]{0:T(512)}) all-reduce(f32[384]{0:T(512)} %get-tuple-element.28, f32[384]{0:T(512)S(1)} %copy-done.27), channel_id=1, replica_groups=mesh['copy'=4,'space'=64] {'copy','space'}, use_global_device_ids=true, to_apply=%region_12.13 | all-reduce | flops 768 | bytes 6144 | tf_op jit(solution)/shard_map/psum | solution.py:123
  615.1 3.4 fusion.17
  (122 shorter events, 61.9 us)
Async XLA Ops:
  7.2 125.9 %copy-start = (bf16[384,1536]{1,0:T(8,128)(2,1)S(1)}, bf16[384,1536]{1,0:T(8,128)(2,1)}, u32[]{:S(2)}) copy-start(bf16[384,1536]{1,0:T(8,128)(2,1)} %param.10) | copy-start | bytes 3538948
  10.5 1.8 copy-start.28
  12.8 3.7 copy-start.25
  16.5 52.1 %all-to-all-start = ((bf16[2,1,4,256,384]{4,0,2,1,3:T(2,128)(2,1)}), bf16[2,1,4,256,384]{4,0,2,1,3:T(2,128)(2,1)}, u32[]{:S(2)}, u32[]{:S(2)}) async-start(bf16[2,1,4,256,384]{4,0,2,1,3:T(2,128)(2,1)} %copy.69), calls=%async_computation | async-start | bytes 3145728 | tf_op jit(solution)/shard_map/all_to_all | solution.py:75
  33.8 40.6 %copy-start.4 = (bf16[1,256,4,384]{1,3,2,0:T(8,128)(2,1)}, bf16[1,256,4,384]{1,3,2,0:T(8,128)(2,1)S(1)}, u32[]{:S(2)}) copy-start(bf16[1,256,4,384]{1,3,2,0:T(8,128)(2,1)S(1)} %copy.124) | copy-start | bytes 2359300
  35.6 38.8 %copy-start.6 = (bf16[1,256,4,384]{1,3,2,0:T(8,128)(2,1)}, bf16[1,256,4,384]{1,3,2,0:T(8,128)(2,1)S(1)}, u32[]{:S(2)}) copy-start(bf16[1,256,4,384]{1,3,2,0:T(8,128)(2,1)S(1)} %copy.126) | copy-start | bytes 2359300
  133.0 15.5 %copy-start.19 = (bf16[1,4,256,384]{3,2,1,0:T(8,128)(2,1)}, bf16[1,4,256,384]{3,2,1,0:T(8,128)(2,1)S(1)}, u32[]{:S(2)}) copy-start(bf16[1,4,256,384]{3,2,1,0:T(8,128)(2,1)S(1)} %multiply_convert_fusion.4) | copy-start | bytes 2359300
  133.0 15.5 %copy-start.17 = (bf16[1,4,256,384]{3,2,1,0:T(8,128)(2,1)S(1)}, bf16[1,4,256,384]{3,2,1,0:T(8,128)(2,1)}, u32[]{:S(2)}) copy-start(bf16[1,4,256,384]{3,2,1,0:T(8,128)(2,1)} %param.8) | copy-start | bytes 2359300
  133.1 15.5 %copy-start.30 = (bf16[1536,384]{1,0:T(8,128)(2,1)S(1)}, bf16[1536,384]{1,0:T(8,128)(2,1)}, u32[]{:S(2)}) copy-start(bf16[1536,384]{1,0:T(8,128)(2,1)} %param.11) | copy-start | bytes 3538948
  151.8 1.9 copy-start.31
  166.2 47.4 %all-to-all-start.2 = ((bf16[2,1,4,256,384]{4,0,2,1,3:T(2,128)(2,1)}), bf16[2,1,4,256,384]{4,0,2,1,3:T(2,128)(2,1)S(1)}, u32[]{:S(2)}, u32[]{:S(2)}) async-start(bf16[2,1,4,256,384]{4,0,2,1,3:T(2,128)(2,1)} %copy.84), calls=%async_computation.2 | async-start | bytes 3145728 | tf_op jit(solution)/shard_map/all_to_all | solution.py:75
  173.9 293.9 %all-reduce.7.cloned.1.call-start = ((), (), s32[]{:S(2)}) async-start(), calls=%async_computation.5 | async-start | bytes 9437184 | tf_op jit(solution)/shard_map/psum | solution.py:123
  174.1 5.2 copy-start.18
  174.1 5.2 copy-start.32
  217.5 4.3 copy-start.5
  217.5 4.3 copy-start.7
  227.0 304.5 %all-to-all-start.3 = ((bf16[2,1,256,4,384]{4,0,3,1,2:T(2,128)(2,1)}), bf16[2,1,256,4,384]{4,0,3,1,2:T(2,128)(2,1)S(1)}, u32[]{:S(2)}, u32[]{:S(2)}) async-start(bf16[2,1,256,4,384]{4,0,3,1,2:T(2,128)(2,1)} %copy.90), calls=%async_computation.3 | async-start | bytes 3145728 | tf_op jit(solution)/shard_map/all_to_all | solution.py:84
  235.3 292.3 %all-reduce.5.cloned.1.call-start = ((), (), s32[]{:S(2)}) async-start(), calls=%async_computation.4 | async-start | bytes 3145728 | tf_op jit(solution)/shard_map/psum | solution.py:119
  235.6 3.9 copy-start.1
  235.6 4.8 copy-start.2
  467.8 3.0 copy-start.10
  533.1 2.6 copy-start.27
  533.1 81.9 %copy-start.8 = (f32[1,4,256,384]{2,3,1,0:T(8,128)S(1)}, f32[1,4,256,384]{2,3,1,0:T(8,128)}, u32[]{:S(2)}) copy-start(f32[1,4,256,384]{2,3,1,0:T(8,128)} %copy.81) | copy-start | bytes 4718596
  618.5 2.4 copy-start.9
  (14 other events, 13.4 us)
Sparse Core Ops, SparseCore 0:
  182.7 285.0 all-reduce.6
  470.7 56.9 all-reduce.4
where the time goes:
time: 639 us; the launch traced here: 629 us
  waiting for transfers between devices  332 us (52%)
  blocking collectives  121 us (19%)
  matrix products  53.9 us (8%)
  local copies, waits for them, and re-layouts  50 us (8%)
  starting transfers between devices  30.3 us (5%)
  other arithmetic  27.3 us (4%)
  between operations  14.7 us (2%)
    psum x1, waiting for transfers between devices, body(): lax.psum((local_sums[0], local_sums[1], local_sums[2], local_sums[3]), ('...  215 us
    psum x1, blocking collectives, body(): lax.psum((local_sums[0], local_sums[1], local_sums[2], local_sums[3]), ('...  76.1 us
    all_to_all x2, waiting for transfers between devices, spectral(): lax.all_to_all(rows, 'space', split_axis=3, concat_axis=2, tiled=True)  61 us
    psum x1, waiting for transfers between devices, body(): lax.psum(filter_terms.astype(jnp.bfloat16), 'copy').astype(jnp.float32)  55.6 us
    all_to_all x1, blocking collectives, spectral(): lax.all_to_all(returned, 'space', split_axis=2, concat_axis=3, tiled=True)  45.2 us
    all_to_all x2, starting transfers between devices, spectral(): lax.all_to_all(rows, 'space', split_axis=3, concat_axis=2, tiled=True)  21.5 us
    unnamed x73, local copies, waits for them, and re-layouts  17.3 us
    dot_general x1, matrix products, body(): preact = jnp.dot(mlp_in, weight_in, preferred_element_type=jnp.float32)  15.5 us
  transfers between devices with their start and end apart: 5, of which 4 were waited for; matrix products, arithmetic and copies ran while one was open for 9% of the time, Pallas kernels for 0%

commit v1 on v0

--- a/solution.py
+++ b/solution.py
@@ -5,6 +5,15 @@
 from jax.sharding import PartitionSpec as P
 
 EPS = 1e-06
+
+
+def _choose_squares(in_array):
+    return jnp.concatenate(
+        lax.all_to_all(
+            jnp.stack(jnp.split(in_array, lax.axis_size("space"), 2), axis=0), "space", 0, 0
+        ),
+        3,
+    )
 
 
 def dft_parts(length):
@@ -81,7 +90,7 @@
     returned = jnp.einsum(
         "qmph,pbhkc->qbmkc", column_table(height, -1), weighted, preferred_element_type=jnp.float32
     ).astype(jnp.bfloat16)
-    back_rows = lax.all_to_all(returned, "space", split_axis=2, concat_axis=3, tiled=True)
+    back_rows = _choose_squares(returned)
     output = jnp.einsum("pkw,pbhkc->bhwc", rows_tab, back_rows, preferred_element_type=jnp.float32)
     return (output, spectrum)
 

time: 639 us -> 623 us (0.975)
  waiting for transfers between devices: 332 us -> 292 us
  local copies, waits for them, and re-layouts: 50 us -> 78.1 us
    unnamed x73 -> x197, local copies, waits for them, and re-layouts: 17.3 us -> 57.1 us
    psum x1, waiting for transfers between devices: 215 us -> 176 us  [body(): lax.psum((local_sums[0], local_sums[1], local_sums[2], local_sums[3]), ('...]
    convert_element_type x2 -> x0, local copies, waits for them, and re-layouts: 7.42 us -> none  [spectral(): returned = jnp.einsum('qmph,pbhkc->qbmkc', column_table(height, -1), weig...]
  transfers between devices with their start and end apart: 5 -> 5, of which waited for: 4 -> 4; matrix products, arithmetic and copies ran while one was open for 9% -> 14% of each run, Pallas kernels for 0% -> 0%
where the time goes in v1:
time: 623 us; the launch traced here: 618 us
  waiting for transfers between devices  292 us (47%)
  blocking collectives  122 us (20%)
  local copies, waits for them, and re-layouts  78.1 us (13%)
  matrix products  52.9 us (8%)
  starting transfers between devices  30.8 us (5%)
  other arithmetic  27.2 us (4%)
  between operations  15 us (2%)
    psum x1, waiting for transfers between devices, body(): lax.psum((local_sums[0], local_sums[1], local_sums[2], local_sums[3]), ('...  176 us
    psum x1, blocking collectives, body(): lax.psum((local_sums[0], local_sums[1], local_sums[2], local_sums[3]), ('...  76.1 us
    all_to_all x2, waiting for transfers between devices, spectral(): lax.all_to_all(rows, 'space', split_axis=3, concat_axis=2, tiled=True)  61 us
    unnamed x197, local copies, waits for them, and re-layouts  57.1 us
    psum x1, waiting for transfers between devices, body(): lax.psum(filter_terms.astype(jnp.bfloat16), 'copy').astype(jnp.float32)  55.6 us
    all_to_all x1, blocking collectives, _choose_squares(): lax.all_to_all(jnp.stack(jnp.split(in_array, lax.axis_size('space'), 2),...  45.4 us
    all_to_all x2, starting transfers between devices, spectral(): lax.all_to_all(rows, 'space', split_axis=3, concat_axis=2, tiled=True)  21.8 us
    dot_general x1, matrix products, body(): preact = jnp.dot(mlp_in, weight_in, preferred_element_type=jnp.float32)  15.5 us
  transfers between devices with their start and end apart: 5, of which 4 were waited for; matrix products, arithmetic and copies ran while one was open for 14% of the time, Pallas kernels for 0%

profile of v1, /device:TPU:1, one launch (start us, length us, event | category | flops | bytes accessed | tf_op | source)
XLA Modules:
  0.0 617.8 jit_solution(5665416679440751984)
XLA Ops:
  13.5 3.0 copy.66
  16.5 14.1 %all-to-all-start = ((bf16[2,1,4,256,384]{4,0,2,1,3:T(2,128)(2,1)}), bf16[2,1,4,256,384]{4,0,2,1,3:T(2,128)(2,1)}, u32[]{:S(2)}, u32[]{:S(2)}) async-start(bf16[2,1,4,256,384]{4,0,2,1,3:T(2,128)(2,1)} %copy.66), calls=%async_computation | async-start | bytes 3145728 | tf_op jit(solution)/shard_map/all_to_all | solution.py:84
  30.6 2.8 fusion.95
  39.0 29.9 %all-to-all-done = bf16[2,1,4,256,384]{4,0,2,1,3:T(2,128)(2,1)} async-done(((bf16[2,1,4,256,384]{4,0,2,1,3:T(2,128)(2,1)}), bf16[2,1,4,256,384]{4,0,2,1,3:T(2,128)(2,1)}, u32[]{:S(2)}, u32[]{:S(2)}) %all-to-all-start) | async-done | bytes 1572896 | tf_op jit(solution)/shard_map/all_to_all | solution.py:84
  78.5 45.4 %all_to_all.40 = bf16[64,2,1,4,4,384]{5,3,1,4,2,0:T(4,128)(2,1)S(1)} all-to-all(bf16[64,2,1,4,4,384]{5,3,1,4,2,0:T(4,128)(2,1)S(1)} %constant_dynamic-update-slice_fusion), channel_id=1, replica_groups=mesh['copy'=4,'space'=64] {'space'}, dimensions={0} | all-to-all | bytes 3145728 | tf_op jit(solution)/shard_map/all_to_all | solution.py:12
  125.7 15.5 %multiply_convert_fusion = (bf16[1024,1536]{1,0:T(8,128)(2,1)}, f32[1024,1536]{1,0:T(8,128)S(1)}, f32[1024,1536]{1,0:T(8,128)S(1)}) fusion(bf16[1024,384]{1,0:T(8,128)(2,1)S(1)} %bitcast.761, bf16[384,1536]{1,0:T(8,128)(2,1)S(1)} %copy-done), kind=kOutput, calls=%fused_computation.3 | convolution fusion | flops 1310195712 | bytes 17694720 | tf_op jit(solution)/shard_map/dot_general | solution.py:106
  141.3 3.3 add_convert_fusion
  150.1 4.0 fusion.42
  154.0 5.0 copy.79
  159.0 7.7 %all-to-all-start.2 = ((bf16[2,1,4,256,384]{4,0,2,1,3:T(2,128)(2,1)}), bf16[2,1,4,256,384]{4,0,2,1,3:T(2,128)(2,1)S(1)}, u32[]{:S(2)}, u32[]{:S(2)}) async-start(bf16[2,1,4,256,384]{4,0,2,1,3:T(2,128)(2,1)} %copy.79), calls=%async_computation.2 | async-start | bytes 3145728 | tf_op jit(solution)/shard_map/all_to_all | solution.py:84
  166.9 5.2 fusion.99
  172.1 3.2 fusion.100
  175.4 31.1 %all-to-all-done.2 = bf16[2,1,4,256,384]{4,0,2,1,3:T(2,128)(2,1)S(1)} async-done(((bf16[2,1,4,256,384]{4,0,2,1,3:T(2,128)(2,1)}), bf16[2,1,4,256,384]{4,0,2,1,3:T(2,128)(2,1)S(1)}, u32[]{:S(2)}, u32[]{:S(2)}) %all-to-all-start.2) | async-done | bytes 1572896 | tf_op jit(solution)/shard_map/all_to_all | solution.py:84
  210.2 4.3 fusion.97
  256.0 8.6 %all-to-all-start.3 = ((bf16[64,2,1,4,4,384]{5,3,1,4,2,0:T(4,128)(2,1)}), bf16[64,2,1,4,4,384]{5,3,1,4,2,0:T(4,128)(2,1)}, u32[]{:S(2)}, u32[]{:S(2)}) async-start(bf16[64,2,1,4,4,384]{5,3,1,4,2,0:T(4,128)(2,1)} %constant_dynamic-update-slice_fusion.64), calls=%async_computation.3 | async-start | bytes 3145728 | tf_op jit(solution)/shard_map/all_to_all | solution.py:12
  264.9 3.4 fusion.59
  273.9 5.2 fusion.98
  280.9 175.6 %all-reduce.7.cloned.1.call-done = (f32[384,1536]{1,0:T(8,128)}, f32[1536,384]{1,0:T(8,128)}) async-done(((f32[384,1536]{1,0:T(8,128)}, f32[1536,384]{1,0:T(8,128)}), (f32[384,1536]{1,0:T(8,128)}, f32[1536,384]{1,0:T(8,128)})) %all-reduce.7.cloned.1.call-update) | async-done | bytes 4718608 | tf_op jit(solution)/shard_map/psum | solution.py:132
  456.6 3.0 multiply_convert_fusion.1
  460.8 55.6 %all-reduce.5.cloned.1.call-done = bf16[2,256,4,384]{1,3,2,0:T(8,128)(2,1)} async-done(((bf16[2,256,4,384]{1,3,2,0:T(8,128)(2,1)}), bf16[2,256,4,384]{1,3,2,0:T(8,128)(2,1)}) %all-reduce.5.cloned.1.call-update) | async-done | bytes 1572880 | tf_op jit(solution)/shard_map/psum | solution.py:128
  516.4 3.9 copy.92
  520.3 4.2 fusion.18
  524.4 76.1 %all-reduce = (f32[384]{0:T(512)}, f32[384]{0:T(512)}) all-reduce(f32[384]{0:T(512)} %get-tuple-element.28, f32[384]{0:T(512)S(1)} %copy-done.27), channel_id=1, replica_groups=mesh['copy'=4,'space'=64] {'copy','space'}, use_global_device_ids=true, to_apply=%region_12.13 | all-reduce | flops 768 | bytes 6144 | tf_op jit(solution)/shard_map/psum | solution.py:132
  603.8 3.4 fusion.17
  (241 shorter events, 89.4 us)
Async XLA Ops:
  7.2 118.5 %copy-start = (bf16[384,1536]{1,0:T(8,128)(2,1)S(1)}, bf16[384,1536]{1,0:T(8,128)(2,1)}, u32[]{:S(2)}) copy-start(bf16[384,1536]{1,0:T(8,128)(2,1)} %param.10) | copy-start | bytes 3538948
  12.8 3.7 copy-start.25
  16.5 52.4 %all-to-all-start = ((bf16[2,1,4,256,384]{4,0,2,1,3:T(2,128)(2,1)}), bf16[2,1,4,256,384]{4,0,2,1,3:T(2,128)(2,1)}, u32[]{:S(2)}, u32[]{:S(2)}) async-start(bf16[2,1,4,256,384]{4,0,2,1,3:T(2,128)(2,1)} %copy.66), calls=%async_computation | async-start | bytes 3145728 | tf_op jit(solution)/shard_map/all_to_all | solution.py:84
  34.1 40.6 %copy-start.4 = (bf16[1,256,4,384]{1,3,2,0:T(8,128)(2,1)}, bf16[1,256,4,384]{1,3,2,0:T(8,128)(2,1)S(1)}, u32[]{:S(2)}) copy-start(bf16[1,256,4,384]{1,3,2,0:T(8,128)(2,1)S(1)} %copy.116) | copy-start | bytes 2359300
  35.9 38.8 %copy-start.6 = (bf16[1,256,4,384]{1,3,2,0:T(8,128)(2,1)}, bf16[1,256,4,384]{1,3,2,0:T(8,128)(2,1)S(1)}, u32[]{:S(2)}) copy-start(bf16[1,256,4,384]{1,3,2,0:T(8,128)(2,1)S(1)} %copy.118) | copy-start | bytes 2359300
  78.4 45.4 %copy-start.17 = (bf16[1,256,256]{2,1,0:T(8,128)(2,1)S(1)}, bf16[1,256,256]{2,1,0:T(8,128)(2,1)}, u32[]{:S(2)}) copy-start(bf16[1,256,256]{2,1,0:T(8,128)(2,1)} %fusion.89) | copy-start | bytes 393220
  78.4 45.4 %copy-start.19 = (bf16[1,256,256]{2,1,0:T(8,128)(2,1)S(1)}, bf16[1,256,256]{2,1,0:T(8,128)(2,1)}, u32[]{:S(2)}) copy-start(bf16[1,256,256]{2,1,0:T(8,128)(2,1)} %multiply_convert_fusion.8) | copy-start | bytes 393220
  125.7 15.6 %copy-start.15 = (bf16[1,4,256,384]{3,2,1,0:T(8,128)(2,1)}, bf16[1,4,256,384]{3,2,1,0:T(8,128)(2,1)S(1)}, u32[]{:S(2)}) copy-start(bf16[1,4,256,384]{3,2,1,0:T(8,128)(2,1)S(1)} %multiply_convert_fusion.4) | copy-start | bytes 2359300
  125.7 15.6 %copy-start.12 = (bf16[1,4,256,384]{3,2,1,0:T(8,128)(2,1)S(1)}, bf16[1,4,256,384]{3,2,1,0:T(8,128)(2,1)}, u32[]{:S(2)}) copy-start(bf16[1,4,256,384]{3,2,1,0:T(8,128)(2,1)} %param.8) | copy-start | bytes 2359300
  125.7 15.6 %copy-start.29 = (bf16[1536,384]{1,0:T(8,128)(2,1)S(1)}, bf16[1536,384]{1,0:T(8,128)(2,1)}, u32[]{:S(2)}) copy-start(bf16[1536,384]{1,0:T(8,128)(2,1)} %param.11) | copy-start | bytes 3538948
  159.0 47.4 %all-to-all-start.2 = ((bf16[2,1,4,256,384]{4,0,2,1,3:T(2,128)(2,1)}), bf16[2,1,4,256,384]{4,0,2,1,3:T(2,128)(2,1)S(1)}, u32[]{:S(2)}, u32[]{:S(2)}) async-start(bf16[2,1,4,256,384]{4,0,2,1,3:T(2,128)(2,1)} %copy.79), calls=%async_computation.2 | async-start | bytes 3145728 | tf_op jit(solution)/shard_map/all_to_all | solution.py:84
  166.7 289.9 %all-reduce.7.cloned.1.call-start = ((), (), s32[]{:S(2)}) async-start(), calls=%async_computation.5 | async-start | bytes 9437184 | tf_op jit(solution)/shard_map/psum | solution.py:132
  166.9 5.2 copy-start.13
  166.9 5.2 copy-start.31
  210.2 4.3 copy-start.5
  210.2 4.3 copy-start.7
  256.0 264.2 %all-to-all-start.3 = ((bf16[64,2,1,4,4,384]{5,3,1,4,2,0:T(4,128)(2,1)}), bf16[64,2,1,4,4,384]{5,3,1,4,2,0:T(4,128)(2,1)}, u32[]{:S(2)}, u32[]{:S(2)}) async-start(bf16[64,2,1,4,4,384]{5,3,1,4,2,0:T(4,128)(2,1)} %constant_dynamic-update-slice_fusion.64), calls=%async_computation.3 | async-start | bytes 3145728 | tf_op jit(solution)/shard_map/all_to_all | solution.py:12
  264.6 251.8 %all-reduce.5.cloned.1.call-start = ((), (), s32[]{:S(2)}) async-start(), calls=%async_computation.4 | async-start | bytes 3145728 | tf_op jit(solution)/shard_map/psum | solution.py:128
  264.9 3.8 copy-start.1
  264.9 4.8 copy-start.2
  456.6 3.0 copy-start.9
  460.8 59.5 %copy-start.26 = (f32[4,256]{1,0:T(4,128)S(1)}, f32[4,256]{1,0:T(4,128)}, u32[]{:S(2)}) copy-start(f32[4,256]{1,0:T(4,128)} %copy-done.25) | copy-start | bytes 12292
  520.3 4.2 copy-start.27
  607.2 2.4 copy-start.8
  (13 other events, 14.5 us)
Sparse Core Ops, SparseCore 0:
  175.5 281.0 all-reduce.6
  459.4 56.9 all-reduce.4
